TPU v7x, 1024 devices: a whole 4x4x32 slice. The times are simulated.
1024 devices in a mesh: outer: 8 (over x, core), inner: 128 (over y, z).
Axes of the slice: x: 4, y: 4, z: 32, core: 2. Of those that a mesh axis runs over, the one named last changes fastest.
Arguments:
- queries: bfloat16 [131072, 4096], P(('outer', 'inner')), may hold values from -200 to 200
- keys: bfloat16 [131072, 1024], P(('outer', 'inner')), may hold values from -6 to 6
- values: bfloat16 [131072, 1024], P(('outer', 'inner')), may hold values from -6 to 6
- lengths: int32 [256], replicated, may hold values from 1 to 1024, as said below
- pack_order: int32 [256], replicated, may hold values from 0 to 255, as said below
Outputs:
- attended: bfloat16 [131072, 4096], P(('outer', 'inner'))
Inputs may be any that keep to these rules, and one draw needn't show every extreme that they name: 256 lengths that sum to 131072; the document packed first, lengths[pack_order[0]], has exactly 1024 tokens. `pack_order`: each of 0 to 255 exactly once.
All inputs are finite; a program needn't handle non-finite values.
Results may differ from a plain program's by a relative error of at most 0.0046.
Values may be sent and summed in bfloat16 or wider, within the bound.
A program may use at most 64 MiB of HBM per device.

v0:
```python
import jax
import jax.numpy as jnp
from jax import lax
from jax.sharding import PartitionSpec as P

HD = 128
HOPS = 8


def shifted(block, axis, distance):
    devices = range(lax.axis_size(axis))
    route = [(i - distance, i) for i in devices if i - distance in devices]
    return lax.ppermute(block, axis, route)


def segment_ids(lengths, pack_order, positions):
    placed = jnp.take(lengths, pack_order)
    doc_starts = jnp.cumsum(placed) - placed
    counted = (doc_starts[None, :] <= positions[:, None]).astype(jnp.int32)
    return jnp.sum(counted, axis=1) - 1


def attend(queries, key_set, value_set, allowed):
    shard_rows = queries.shape[0]
    kv_heads = key_set.shape[1] // HD
    group_size = queries.shape[1] // key_set.shape[1]
    width = group_size * HD
    inv_root = jnp.sqrt(jnp.float32(HD))

    def per_group(head_group, output):
        query_part = lax.dynamic_slice_in_dim(queries, head_group * width, width, 1).reshape(
            shard_rows, group_size, HD
        )
        key_part = lax.dynamic_slice_in_dim(key_set, head_group * HD, HD, 1)
        value_part = lax.dynamic_slice_in_dim(value_set, head_group * HD, HD, 1)
        scores = (
            jnp.einsum("tjd,kd->jtk", query_part, key_part, preferred_element_type=jnp.float32)
            / inv_root
        )
        scores = jnp.where(allowed[None], scores, -jnp.inf)
        largest = jnp.max(scores, axis=-1, keepdims=True)
        exps = jnp.exp(scores - largest)
        weights = (exps / jnp.sum(exps, axis=-1, keepdims=True)).astype(jnp.bfloat16)
        mixed = jnp.einsum("jtk,kd->tjd", weights, value_part, preferred_element_type=jnp.float32)
        mixed = mixed.reshape(shard_rows, width).astype(jnp.bfloat16)
        return lax.dynamic_update_slice_in_dim(output, mixed, head_group * width, 1)

    initial = jnp.zeros(queries.shape, jnp.bfloat16)
    return lax.fori_loop(0, kv_heads, per_group, initial)


def shards(queries, keys, values, lengths, pack_order):
    shard_rows = queries.shape[0]
    device = lax.axis_index(("outer", "inner"))
    first_row = device * shard_rows
    received = []
    passed = (keys, values)
    for distance in range(1, HOPS + 1):
        passed = shifted((passed[0], passed[1]), ("outer", "inner"), 1)
        received.append(passed)
    ordered = received[::-1]
    key_all = jnp.concatenate([pair[0] for pair in ordered] + [keys], axis=0)
    value_all = jnp.concatenate([pair[1] for pair in ordered] + [values], axis=0)
    window = key_all.shape[0]
    query_pos = first_row + jnp.arange(shard_rows, dtype=jnp.int32)
    key_pos = first_row - HOPS * shard_rows + jnp.arange(window, dtype=jnp.int32)
    query_seg = segment_ids(lengths, pack_order, query_pos)
    key_seg = segment_ids(lengths, pack_order, key_pos)
    allowed = (
        (key_pos[None, :] >= 0)
        & (key_pos[None, :] <= query_pos[:, None])
        & (key_seg[None, :] == query_seg[:, None])
    )
    attended = attend(queries, key_all, value_all, allowed)
    return attended


def solution(mesh):
    in_specs = (
        P(("outer", "inner"), None),
        P(("outer", "inner"), None),
        P(("outer", "inner"), None),
        P(),
        P(),
    )
    out_specs = P(("outer", "inner"), None)
    return jax.shard_map(shards, mesh=mesh, in_specs=in_specs, out_specs=out_specs, check_vma=False)
```

profile of v0, /device:TPU:6, one launch (start us, length us, event | category | flops | bytes accessed | tf_op | source)
XLA Modules:
  0.0 193.2 jit_solution(6510598279278660000)
XLA Ops:
  1.1 3.8 %collective-permute-start = (bf16[128,1024]{0,1:T(8,128)(2,1)S(1)}, bf16[128,1024]{0,1:T(8,128)(2,1)S(1)}, u32[]{:S(2)}, u32[]{:S(2)}) collective-permute-start(bf16[128,1024]{0,1:T(8,128)(2,1)S(1)} %copy.18), channel_id=1, source_target_pairs={{0,1},{1,2},{2,3},{3,4},{4,5},{5,6},{6,7},{7,8},{8,9},{9,10},{10,1... | collective-permute-start | bytes 786440 | tf_op jit(solution)/shard_map/ppermute | solution.py:13
  5.0 3.8 %collective-permute-start.8 = (bf16[128,1024]{1,0:T(8,128)(2,1)}, bf16[128,1024]{1,0:T(8,128)(2,1)S(1)}, u32[]{:S(2)}, u32[]{:S(2)}) collective-permute-start(bf16[128,1024]{1,0:T(8,128)(2,1)} %param.10), channel_id=1, source_target_pairs={{0,1},{1,2},{2,3},{3,4},{4,5},{5,6},{6,7},{7,8},{8,9},{9,10},{10,1... | collective-permute-start | bytes 786440 | tf_op jit(solution)/shard_map/ppermute | solution.py:13
  8.8 20.7 %collective-permute-done = bf16[128,1024]{0,1:T(8,128)(2,1)S(1)} collective-permute-done((bf16[128,1024]{0,1:T(8,128)(2,1)S(1)}, bf16[128,1024]{0,1:T(8,128)(2,1)S(1)}, u32[]{:S(2)}, u32[]{:S(2)}) %collective-permute-start) | collective-permute-done | bytes 262176 | tf_op jit(solution)/shard_map/ppermute | solution.py:13
  31.5 3.0 %collective-permute-done.8 = bf16[128,1024]{1,0:T(8,128)(2,1)S(1)} collective-permute-done((bf16[128,1024]{1,0:T(8,128)(2,1)}, bf16[128,1024]{1,0:T(8,128)(2,1)S(1)}, u32[]{:S(2)}, u32[]{:S(2)}) %collective-permute-start.8) | collective-permute-done | bytes 262176 | tf_op jit(solution)/shard_map/ppermute | solution.py:13
  34.4 1.9 collective-permute-start.9
  36.4 9.1 %collective-permute-done.1 = bf16[128,1024]{0,1:T(8,128)(2,1)S(1)} collective-permute-done((bf16[128,1024]{0,1:T(8,128)(2,1)S(1)}, bf16[128,1024]{0,1:T(8,128)(2,1)S(1)}, u32[]{:S(2)}, u32[]{:S(2)}) %collective-permute-start.1) | collective-permute-done | bytes 262176 | tf_op jit(solution)/shard_map/ppermute | solution.py:13
  48.1 2.3 %collective-permute-done.9 = bf16[128,1024]{1,0:T(8,128)(2,1)S(1)} collective-permute-done((bf16[128,1024]{1,0:T(8,128)(2,1)S(1)}, bf16[128,1024]{1,0:T(8,128)(2,1)S(1)}, u32[]{:S(2)}, u32[]{:S(2)}) %collective-permute-start.9) | collective-permute-done | bytes 262176 | tf_op jit(solution)/shard_map/ppermute | solution.py:13
  50.4 1.9 collective-permute-start.10
  52.3 7.2 %collective-permute-done.2 = bf16[128,1024]{0,1:T(8,128)(2,1)S(1)} collective-permute-done((bf16[128,1024]{0,1:T(8,128)(2,1)S(1)}, bf16[128,1024]{0,1:T(8,128)(2,1)S(1)}, u32[]{:S(2)}, u32[]{:S(2)}) %collective-permute-start.2) | collective-permute-done | bytes 262176 | tf_op jit(solution)/shard_map/ppermute | solution.py:13
  59.6 1.9 collective-permute-start.3
  61.5 1.9 %gather_fusion = s32[256]{0:T(256)S(1)} fusion(s32[256]{0:T(256)S(1)} %copy-done, s32[1024]{0:T(1024)S(1)} %pad_clamp_fusion), kind=kCustom, calls=%fused_computation.clone | custom fusion | bytes 3072 | tf_op jit(solution)/shard_map/jit(_take)/gather | solution.py:17
  67.2 5.5 %collective-permute-done.3 = bf16[128,1024]{0,1:T(8,128)(2,1)S(1)} collective-permute-done((bf16[128,1024]{0,1:T(8,128)(2,1)S(1)}, bf16[128,1024]{0,1:T(8,128)(2,1)S(1)}, u32[]{:S(2)}, u32[]{:S(2)}) %collective-permute-start.3) | collective-permute-done | bytes 262176 | tf_op jit(solution)/shard_map/ppermute | solution.py:13
  75.5 3.0 %collective-permute-done.11 = bf16[128,1024]{1,0:T(8,128)(2,1)S(1)} collective-permute-done((bf16[128,1024]{1,0:T(8,128)(2,1)S(1)}, bf16[128,1024]{1,0:T(8,128)(2,1)S(1)}, u32[]{:S(2)}, u32[]{:S(2)}) %collective-permute-start.11) | collective-permute-done | bytes 262176 | tf_op jit(solution)/shard_map/ppermute | solution.py:13
  80.4 6.1 %collective-permute-done.4 = bf16[128,1024]{0,1:T(8,128)(2,1)S(1)} collective-permute-done((bf16[128,1024]{0,1:T(8,128)(2,1)S(1)}, bf16[128,1024]{0,1:T(8,128)(2,1)S(1)}, u32[]{:S(2)}, u32[]{:S(2)}) %collective-permute-start.4) | collective-permute-done | bytes 262176 | tf_op jit(solution)/shard_map/ppermute | solution.py:13
  86.5 1.9 collective-permute-start.5
  88.8 4.7 %collective-permute-done.12 = bf16[128,1024]{1,0:T(8,128)(2,1)S(1)} collective-permute-done((bf16[128,1024]{1,0:T(8,128)(2,1)S(1)}, bf16[128,1024]{1,0:T(8,128)(2,1)S(1)}, u32[]{:S(2)}, u32[]{:S(2)}) %collective-permute-start.12) | collective-permute-done | bytes 262176 | tf_op jit(solution)/shard_map/ppermute | solution.py:13
  95.5 6.2 %collective-permute-done.5 = bf16[128,1024]{0,1:T(8,128)(2,1)} collective-permute-done((bf16[128,1024]{0,1:T(8,128)(2,1)S(1)}, bf16[128,1024]{0,1:T(8,128)(2,1)}, u32[]{:S(2)}, u32[]{:S(2)}) %collective-permute-start.5) | collective-permute-done | bytes 262176 | tf_op jit(solution)/shard_map/ppermute | solution.py:13
  101.7 1.9 collective-permute-start.6
  103.8 3.9 %collective-permute-done.13 = bf16[128,1024]{1,0:T(8,128)(2,1)S(1)} collective-permute-done((bf16[128,1024]{1,0:T(8,128)(2,1)S(1)}, bf16[128,1024]{1,0:T(8,128)(2,1)S(1)}, u32[]{:S(2)}, u32[]{:S(2)}) %collective-permute-start.13) | collective-permute-done | bytes 262176 | tf_op jit(solution)/shard_map/ppermute | solution.py:13
  107.7 1.9 collective-permute-start.14
  109.6 8.3 %collective-permute-done.6 = bf16[128,1024]{0,1:T(8,128)(2,1)} collective-permute-done((bf16[128,1024]{0,1:T(8,128)(2,1)}, bf16[128,1024]{0,1:T(8,128)(2,1)}, u32[]{:S(2)}, u32[]{:S(2)}) %collective-permute-start.6) | collective-permute-done | bytes 262176 | tf_op jit(solution)/shard_map/ppermute | solution.py:13
  117.9 1.9 collective-permute-start.7
  123.6 6.5 %collective-permute-done.7 = bf16[128,1024]{0,1:T(8,128)(2,1)} collective-permute-done((bf16[128,1024]{0,1:T(8,128)(2,1)}, bf16[128,1024]{0,1:T(8,128)(2,1)}, u32[]{:S(2)}, u32[]{:S(2)}) %collective-permute-start.7) | collective-permute-done | bytes 262176 | tf_op jit(solution)/shard_map/ppermute | solution.py:13
  141.6 50.7 %while.14 = (s32[]{:T(128)}, bf16[128,4096]{1,0:T(8,128)(2,1)S(1)}, bf16[1152,1024]{0,1:T(8,128)(2,1)}, bf16[1152,1024]{1,0:T(8,128)(2,1)}, bf16[128,4096]{1,0:T...) while((s32[]{:T(128)}, bf16[128,4096]{1,0:T(8,128)(2,1)S(1)}, ...), condition=%wide.region_7.9_spmd.clone, body=%wide.region_4.8_spmd.clone.sunk | while | flops 458951424 | bytes 2785661 | solution.py:49
  145.5 2.2 %fusion.53 = bf16[128,4,128]{2,0,1:T(8,128)(2,1)S(1)} fusion(f32[4,128]{1,0:T(4,128)S(1)} %fusion.52, bf16[1152,1024]{0,1:T(8,128)(2,1)} %get-tuple-element.278, s32[]{:T(128)S(6)} %select_n.64, bf16[128,4,128]{0,2,1:T(8,128)(2,1)S(1)} %bitcast.59, pred[128,1152]{0,1:T(8,128)(4,1)S(1)} %compare_and_fusion.2, bf16[1152,1024]{1,0:T(8,128)(2,1)} %get-tuple-element.279), kind=kOutput, calls=%fused_computation.10.clone.1 | convolution fusion | flops 305006208 | bytes 1002496 | tf_op jit(solution)/shard_map/while/body/eval_jaxpr/jtk,kd->tjd/dot_general | solution.py:44
  151.9 2.2 %fusion.53 = bf16[128,4,128]{2,0,1:T(8,128)(2,1)S(1)} fusion(f32[4,128]{1,0:T(4,128)S(1)} %fusion.52, bf16[1152,1024]{0,1:T(8,128)(2,1)} %get-tuple-element.278, s32[]{:T(128)S(6)} %select_n.64, bf16[128,4,128]{0,2,1:T(8,128)(2,1)S(1)} %bitcast.59, pred[128,1152]{0,1:T(8,128)(4,1)S(1)} %compare_and_fusion.2, bf16[1152,1024]{1,0:T(8,128)(2,1)} %get-tuple-element.279), kind=kOutput, calls=%fused_computation.10.clone.1 | convolution fusion | flops 305006208 | bytes 1002496 | tf_op jit(solution)/shard_map/while/body/eval_jaxpr/jtk,kd->tjd/dot_general | solution.py:44
  158.2 2.2 %fusion.53 = bf16[128,4,128]{2,0,1:T(8,128)(2,1)S(1)} fusion(f32[4,128]{1,0:T(4,128)S(1)} %fusion.52, bf16[1152,1024]{0,1:T(8,128)(2,1)} %get-tuple-element.278, s32[]{:T(128)S(6)} %select_n.64, bf16[128,4,128]{0,2,1:T(8,128)(2,1)S(1)} %bitcast.59, pred[128,1152]{0,1:T(8,128)(4,1)S(1)} %compare_and_fusion.2, bf16[1152,1024]{1,0:T(8,128)(2,1)} %get-tuple-element.279), kind=kOutput, calls=%fused_computation.10.clone.1 | convolution fusion | flops 305006208 | bytes 1002496 | tf_op jit(solution)/shard_map/while/body/eval_jaxpr/jtk,kd->tjd/dot_general | solution.py:44
  164.5 2.2 %fusion.53 = bf16[128,4,128]{2,0,1:T(8,128)(2,1)S(1)} fusion(f32[4,128]{1,0:T(4,128)S(1)} %fusion.52, bf16[1152,1024]{0,1:T(8,128)(2,1)} %get-tuple-element.278, s32[]{:T(128)S(6)} %select_n.64, bf16[128,4,128]{0,2,1:T(8,128)(2,1)S(1)} %bitcast.59, pred[128,1152]{0,1:T(8,128)(4,1)S(1)} %compare_and_fusion.2, bf16[1152,1024]{1,0:T(8,128)(2,1)} %get-tuple-element.279), kind=kOutput, calls=%fused_computation.10.clone.1 | convolution fusion | flops 305006208 | bytes 1002496 | tf_op jit(solution)/shard_map/while/body/eval_jaxpr/jtk,kd->tjd/dot_general | solution.py:44
  170.9 2.2 %fusion.53 = bf16[128,4,128]{2,0,1:T(8,128)(2,1)S(1)} fusion(f32[4,128]{1,0:T(4,128)S(1)} %fusion.52, bf16[1152,1024]{0,1:T(8,128)(2,1)} %get-tuple-element.278, s32[]{:T(128)S(6)} %select_n.64, bf16[128,4,128]{0,2,1:T(8,128)(2,1)S(1)} %bitcast.59, pred[128,1152]{0,1:T(8,128)(4,1)S(1)} %compare_and_fusion.2, bf16[1152,1024]{1,0:T(8,128)(2,1)} %get-tuple-element.279), kind=kOutput, calls=%fused_computation.10.clone.1 | convolution fusion | flops 305006208 | bytes 1002496 | tf_op jit(solution)/shard_map/while/body/eval_jaxpr/jtk,kd->tjd/dot_general | solution.py:44
  177.2 2.2 %fusion.53 = bf16[128,4,128]{2,0,1:T(8,128)(2,1)S(1)} fusion(f32[4,128]{1,0:T(4,128)S(1)} %fusion.52, bf16[1152,1024]{0,1:T(8,128)(2,1)} %get-tuple-element.278, s32[]{:T(128)S(6)} %select_n.64, bf16[128,4,128]{0,2,1:T(8,128)(2,1)S(1)} %bitcast.59, pred[128,1152]{0,1:T(8,128)(4,1)S(1)} %compare_and_fusion.2, bf16[1152,1024]{1,0:T(8,128)(2,1)} %get-tuple-element.279), kind=kOutput, calls=%fused_computation.10.clone.1 | convolution fusion | flops 305006208 | bytes 1002496 | tf_op jit(solution)/shard_map/while/body/eval_jaxpr/jtk,kd->tjd/dot_general | solution.py:44
  183.6 2.2 %fusion.53 = bf16[128,4,128]{2,0,1:T(8,128)(2,1)S(1)} fusion(f32[4,128]{1,0:T(4,128)S(1)} %fusion.52, bf16[1152,1024]{0,1:T(8,128)(2,1)} %get-tuple-element.278, s32[]{:T(128)S(6)} %select_n.64, bf16[128,4,128]{0,2,1:T(8,128)(2,1)S(1)} %bitcast.59, pred[128,1152]{0,1:T(8,128)(4,1)S(1)} %compare_and_fusion.2, bf16[1152,1024]{1,0:T(8,128)(2,1)} %get-tuple-element.279), kind=kOutput, calls=%fused_computation.10.clone.1 | convolution fusion | flops 305006208 | bytes 1002496 | tf_op jit(solution)/shard_map/while/body/eval_jaxpr/jtk,kd->tjd/dot_general | solution.py:44
  189.9 2.2 %fusion.53 = bf16[128,4,128]{2,0,1:T(8,128)(2,1)S(1)} fusion(f32[4,128]{1,0:T(4,128)S(1)} %fusion.52, bf16[1152,1024]{0,1:T(8,128)(2,1)} %get-tuple-element.278, s32[]{:T(128)S(6)} %select_n.64, bf16[128,4,128]{0,2,1:T(8,128)(2,1)S(1)} %bitcast.59, pred[128,1152]{0,1:T(8,128)(4,1)S(1)} %compare_and_fusion.2, bf16[1152,1024]{1,0:T(8,128)(2,1)} %get-tuple-element.279), kind=kOutput, calls=%fused_computation.10.clone.1 | convolution fusion | flops 305006208 | bytes 1002496 | tf_op jit(solution)/shard_map/while/body/eval_jaxpr/jtk,kd->tjd/dot_general | solution.py:44
  (101 shorter events, 65.1 us)
Async XLA Ops:
  0.0 61.5 %copy-start = (s32[256]{0:T(256)S(1)}, s32[256]{0:T(256)}, u32[]{:S(2)}) copy-start(s32[256]{0:T(256)} %param.12) | copy-start | bytes 3076
  1.1 28.4 %collective-permute-start = (bf16[128,1024]{0,1:T(8,128)(2,1)S(1)}, bf16[128,1024]{0,1:T(8,128)(2,1)S(1)}, u32[]{:S(2)}, u32[]{:S(2)}) collective-permute-start(bf16[128,1024]{0,1:T(8,128)(2,1)S(1)} %copy.18), channel_id=1, source_target_pairs={{0,1},{1,2},{2,3},{3,4},{4,5},{5,6},{6,7},{7,8},{8,9},{9,10},{10,1... | collective-permute-start | bytes 786440 | tf_op jit(solution)/shard_map/ppermute | solution.py:13
  5.0 29.5 %collective-permute-start.8 = (bf16[128,1024]{1,0:T(8,128)(2,1)}, bf16[128,1024]{1,0:T(8,128)(2,1)S(1)}, u32[]{:S(2)}, u32[]{:S(2)}) collective-permute-start(bf16[128,1024]{1,0:T(8,128)(2,1)} %param.10), channel_id=1, source_target_pairs={{0,1},{1,2},{2,3},{3,4},{4,5},{5,6},{6,7},{7,8},{8,9},{9,10},{10,1... | collective-permute-start | bytes 786440 | tf_op jit(solution)/shard_map/ppermute | solution.py:13
  29.6 15.9 %collective-permute-start.1 = (bf16[128,1024]{0,1:T(8,128)(2,1)S(1)}, bf16[128,1024]{0,1:T(8,128)(2,1)S(1)}, u32[]{:S(2)}, u32[]{:S(2)}) collective-permute-start(bf16[128,1024]{0,1:T(8,128)(2,1)S(1)} %collective-permute-done), channel_id=1, source_target_pairs={{0,1},{1,2},{2,3},{3,4},{4,5},{5,6},{6,7},{7,8},{8,9},{9,10},{10,1... | collective-permute-start | bytes 786440 | tf_op jit(solution)/shard_map/ppermute | solution.py:13
  34.4 15.9 %collective-permute-start.9 = (bf16[128,1024]{1,0:T(8,128)(2,1)S(1)}, bf16[128,1024]{1,0:T(8,128)(2,1)S(1)}, u32[]{:S(2)}, u32[]{:S(2)}) collective-permute-start(bf16[128,1024]{1,0:T(8,128)(2,1)S(1)} %collective-permute-done.8), channel_id=1, source_target_pairs={{0,1},{1,2},{2,3},{3,4},{4,5},{5,6},{6,7},{7,8},{8,9},{9,10},{10,1... | collective-permute-start | bytes 786440 | tf_op jit(solution)/shard_map/ppermute | solution.py:13
  45.5 14.1 %collective-permute-start.2 = (bf16[128,1024]{0,1:T(8,128)(2,1)S(1)}, bf16[128,1024]{0,1:T(8,128)(2,1)S(1)}, u32[]{:S(2)}, u32[]{:S(2)}) collective-permute-start(bf16[128,1024]{0,1:T(8,128)(2,1)S(1)} %collective-permute-done.1), channel_id=1, source_target_pairs={{0,1},{1,2},{2,3},{3,4},{4,5},{5,6},{6,7},{7,8},{8,9},{9,10},{10,1... | collective-permute-start | bytes 786440 | tf_op jit(solution)/shard_map/ppermute | solution.py:13
  50.4 14.9 %collective-permute-start.10 = (bf16[128,1024]{1,0:T(8,128)(2,1)S(1)}, bf16[128,1024]{1,0:T(8,128)(2,1)S(1)}, u32[]{:S(2)}, u32[]{:S(2)}) collective-permute-start(bf16[128,1024]{1,0:T(8,128)(2,1)S(1)} %collective-permute-done.9), channel_id=1, source_target_pairs={{0,1},{1,2},{2,3},{3,4},{4,5},{5,6},{6,7},{7,8},{8,9},{9,10},{10,1... | collective-permute-start | bytes 786440 | tf_op jit(solution)/shard_map/ppermute | solution.py:13
  59.6 13.1 %collective-permute-start.3 = (bf16[128,1024]{0,1:T(8,128)(2,1)S(1)}, bf16[128,1024]{0,1:T(8,128)(2,1)S(1)}, u32[]{:S(2)}, u32[]{:S(2)}) collective-permute-start(bf16[128,1024]{0,1:T(8,128)(2,1)S(1)} %collective-permute-done.2), channel_id=1, source_target_pairs={{0,1},{1,2},{2,3},{3,4},{4,5},{5,6},{6,7},{7,8},{8,9},{9,10},{10,1... | collective-permute-start | bytes 786440 | tf_op jit(solution)/shard_map/ppermute | solution.py:13
  65.3 13.2 %collective-permute-start.11 = (bf16[128,1024]{1,0:T(8,128)(2,1)S(1)}, bf16[128,1024]{1,0:T(8,128)(2,1)S(1)}, u32[]{:S(2)}, u32[]{:S(2)}) collective-permute-start(bf16[128,1024]{1,0:T(8,128)(2,1)S(1)} %collective-permute-done.10), channel_id=1, source_target_pairs={{0,1},{1,2},{2,3},{3,4},{4,5},{5,6},{6,7},{7,8},{8,9},{9,10},{10,1... | collective-permute-start | bytes 786440 | tf_op jit(solution)/shard_map/ppermute | solution.py:13
  72.7 13.8 %collective-permute-start.4 = (bf16[128,1024]{0,1:T(8,128)(2,1)S(1)}, bf16[128,1024]{0,1:T(8,128)(2,1)S(1)}, u32[]{:S(2)}, u32[]{:S(2)}) collective-permute-start(bf16[128,1024]{0,1:T(8,128)(2,1)S(1)} %collective-permute-done.3), channel_id=1, source_target_pairs={{0,1},{1,2},{2,3},{3,4},{4,5},{5,6},{6,7},{7,8},{8,9},{9,10},{10,1... | collective-permute-start | bytes 786440 | tf_op jit(solution)/shard_map/ppermute | solution.py:13
  78.5 15.1 %collective-permute-start.12 = (bf16[128,1024]{1,0:T(8,128)(2,1)S(1)}, bf16[128,1024]{1,0:T(8,128)(2,1)S(1)}, u32[]{:S(2)}, u32[]{:S(2)}) collective-permute-start(bf16[128,1024]{1,0:T(8,128)(2,1)S(1)} %collective-permute-done.11), channel_id=1, source_target_pairs={{0,1},{1,2},{2,3},{3,4},{4,5},{5,6},{6,7},{7,8},{8,9},{9,10},{10,1... | collective-permute-start | bytes 786440 | tf_op jit(solution)/shard_map/ppermute | solution.py:13
  86.5 15.2 %collective-permute-start.5 = (bf16[128,1024]{0,1:T(8,128)(2,1)S(1)}, bf16[128,1024]{0,1:T(8,128)(2,1)}, u32[]{:S(2)}, u32[]{:S(2)}) collective-permute-start(bf16[128,1024]{0,1:T(8,128)(2,1)S(1)} %collective-permute-done.4), channel_id=1, source_target_pairs={{0,1},{1,2},{2,3},{3,4},{4,5},{5,6},{6,7},{7,8},{8,9},{9,10},{10,1... | collective-permute-start | bytes 786440 | tf_op jit(solution)/shard_map/ppermute | solution.py:13
  93.5 14.1 %collective-permute-start.13 = (bf16[128,1024]{1,0:T(8,128)(2,1)S(1)}, bf16[128,1024]{1,0:T(8,128)(2,1)S(1)}, u32[]{:S(2)}, u32[]{:S(2)}) collective-permute-start(bf16[128,1024]{1,0:T(8,128)(2,1)S(1)} %collective-permute-done.12), channel_id=1, source_target_pairs={{0,1},{1,2},{2,3},{3,4},{4,5},{5,6},{6,7},{7,8},{8,9},{9,10},{10,1... | collective-permute-start | bytes 786440 | tf_op jit(solution)/shard_map/ppermute | solution.py:13
  101.7 16.2 %collective-permute-start.6 = (bf16[128,1024]{0,1:T(8,128)(2,1)}, bf16[128,1024]{0,1:T(8,128)(2,1)}, u32[]{:S(2)}, u32[]{:S(2)}) collective-permute-start(bf16[128,1024]{0,1:T(8,128)(2,1)} %collective-permute-done.5), channel_id=1, source_target_pairs={{0,1},{1,2},{2,3},{3,4},{4,5},{5,6},{6,7},{7,8},{8,9},{9,10},{10,1... | collective-permute-start | bytes 786440 | tf_op jit(solution)/shard_map/ppermute | solution.py:13
  107.7 14.0 %collective-permute-start.14 = (bf16[128,1024]{1,0:T(8,128)(2,1)S(1)}, bf16[128,1024]{1,0:T(8,128)(2,1)}, u32[]{:S(2)}, u32[]{:S(2)}) collective-permute-start(bf16[128,1024]{1,0:T(8,128)(2,1)S(1)} %collective-permute-done.13), channel_id=1, source_target_pairs={{0,1},{1,2},{2,3},{3,4},{4,5},{5,6},{6,7},{7,8},{8,9},{9,10},{10,1... | collective-permute-start | bytes 786440 | tf_op jit(solution)/shard_map/ppermute | solution.py:13
  117.9 12.2 %collective-permute-start.7 = (bf16[128,1024]{0,1:T(8,128)(2,1)}, bf16[128,1024]{0,1:T(8,128)(2,1)}, u32[]{:S(2)}, u32[]{:S(2)}) collective-permute-start(bf16[128,1024]{0,1:T(8,128)(2,1)} %collective-permute-done.6), channel_id=1, source_target_pairs={{0,1},{1,2},{2,3},{3,4},{4,5},{5,6},{6,7},{7,8},{8,9},{9,10},{10,1... | collective-permute-start | bytes 786440 | tf_op jit(solution)/shard_map/ppermute | solution.py:13
  121.7 12.1 %collective-permute-start.15 = (bf16[128,1024]{1,0:T(8,128)(2,1)}, bf16[128,1024]{1,0:T(8,128)(2,1)S(1)}, u32[]{:S(2)}, u32[]{:S(2)}) collective-permute-start(bf16[128,1024]{1,0:T(8,128)(2,1)} %collective-permute-done.14), channel_id=1, source_target_pairs={{0,1},{1,2},{2,3},{3,4},{4,5},{5,6},{6,7},{7,8},{8,9},{9,10},{10,1... | collective-permute-start | bytes 786440 | tf_op jit(solution)/shard_map/ppermute | solution.py:13
  133.5 7.2 %copy-start.2 = (bf16[128,1024]{1,0:T(8,128)(2,1)S(1)}, bf16[128,1024]{1,0:T(8,128)(2,1)}, u32[]{:S(2)}) copy-start(bf16[128,1024]{1,0:T(8,128)(2,1)} %param.10) | copy-start | bytes 786436
  133.6 7.1 %copy-start.3 = (bf16[1152,1024]{0,1:T(8,128)(2,1)}, bf16[1152,1024]{0,1:T(8,128)(2,1)S(1)}, u32[]{:S(2)}) copy-start(bf16[1152,1024]{0,1:T(8,128)(2,1)S(1)} %constant_dynamic-update-slice_fusion.1) | copy-start | bytes 7077892
  192.3 1.0 copy-start.1
where the time goes:
time: 195 us; the launch traced here: 193 us
  waiting for transfers between devices  89.4 us (46%)
  starting transfers between devices  34.4 us (18%)
  matrix products  32.4 us (17%)
  local copies, waits for them, and re-layouts  24.7 us (13%)
  other arithmetic  11.5 us (6%)
    ppermute x16, waiting for transfers between devices, shifted(): return lax.ppermute(block, axis, route)  89.4 us
    ppermute x16, starting transfers between devices, shifted(): return lax.ppermute(block, axis, route)  34.4 us
    dot_general x8, matrix products, per_group(): jnp.einsum('jtk,kd->tjd', weights, value_part, preferred_element_type=jnp...  17.7 us
    sub x8, matrix products, per_group(): exps = jnp.exp(scores - largest)  14.7 us
    unnamed x25, local copies, waits for them, and re-layouts  12.4 us
    and x8, other arithmetic, shards(): (key_pos[None, :] >= 0) & (key_pos[None, :] <= query_pos[:, None])  8.44 us
    dynamic_slice x16, local copies, waits for them, and re-layouts, per_group(): lax.dynamic_slice_in_dim(queries, head_group * width, width, 1)  8.29 us
  transfers between devices with their start and end apart: 16, of which 16 were waited for; matrix products, arithmetic and copies ran while one was open for 4% of the time, Pallas kernels for 0%

commit v1 on v0

v1 whole, which is shorter than its diff:
```python
import functools
import math

import jax
import jax.numpy as jnp
from jax import lax
from jax.experimental import pallas as pl
from jax.experimental.pallas import tpu as pltpu
from jax.sharding import PartitionSpec as P

HD = 128
HOPS = 8
MESH = pl.DeviceIdType.MESH
SCALE = math.log2(math.e) / math.sqrt(HD)


def kernel(sizes, q_hbm, k_hbm, v_hbm, len_hbm, ord_hbm, o_hbm,
           len_ref, ord_ref, q_buf, o_buf, kv, acc, m_buf, l_buf, rel_buf, doc_sem, q_sem, in_sem, out_sem, send_sem, recv_sem):
    n_outer, n_inner = sizes
    rows = q_hbm.shape[0]
    kv_heads = k_hbm.shape[1] // HD
    group = q_hbm.shape[1] // k_hbm.shape[1]
    ndoc = len_hbm.shape[1]
    outer, inner = lax.axis_index("outer"), lax.axis_index("inner")
    device = outer * n_inner + inner
    total = n_outer * n_inner
    after = lax.rem(device + 1, total)
    before = lax.rem(device + total - 1, total)
    right = (after // n_inner, lax.rem(after, n_inner))
    left = (before // n_inner, lax.rem(before, n_inner))

    def load(h, part):
        source = k_hbm if part == 0 else v_hbm
        columns = pl.ds(pl.multiple_of(h * HD, HD), HD)
        return pltpu.make_async_copy(source.at[:, columns], kv.at[0, h, part], in_sem.at[h, part])

    def give(h):
        columns = pl.ds(pl.multiple_of(h * group * HD, group * HD), group * HD)
        return pltpu.make_async_copy(o_buf.at[:, columns], o_hbm.at[:, columns], out_sem.at[h])

    def hop(d, h):
        return pltpu.make_async_remote_copy(
            src_ref=kv.at[d, h], dst_ref=kv.at[d + 1, h],
            send_sem=send_sem.at[d, h], recv_sem=recv_sem.at[d, h],
            device_id=right, device_id_type=MESH)

    @pl.loop(0, kv_heads)
    def _(h):
        load(h, 0).start()
        load(h, 1).start()

    len_copy = pltpu.make_async_copy(len_hbm, len_ref, doc_sem.at[0])
    ord_copy = pltpu.make_async_copy(ord_hbm, ord_ref, doc_sem.at[1])
    len_copy.start()
    ord_copy.start()
    q_copy = pltpu.make_async_copy(q_hbm, q_buf, q_sem)
    q_copy.start()

    barrier = pltpu.get_barrier_semaphore()
    for neighbour in (left, right):
        pl.semaphore_signal(barrier, inc=1, device_id=neighbour, device_id_type=MESH)
    pl.semaphore_wait(barrier, 2)

    @pl.loop(0, kv_heads)
    def _(h):
        load(h, 0).wait()
        load(h, 1).wait()
        hop(0, h).start()

    len_copy.wait()
    ord_copy.wait()
    sub = lax.broadcasted_iota(jnp.int32, (ndoc, ndoc), 0)
    lane = lax.broadcasted_iota(jnp.int32, (ndoc, ndoc), 1)
    lengths = jnp.broadcast_to(len_ref[...], (ndoc, ndoc))
    order = jnp.broadcast_to(ord_ref[...], (ndoc, ndoc))
    zero = jnp.zeros((ndoc, ndoc), jnp.float32)
    by_row = jnp.sum(jnp.where(sub == lane, lengths.astype(jnp.float32), zero), axis=1, keepdims=True)
    placed = jnp.sum(jnp.where(sub == order, jnp.broadcast_to(by_row, (ndoc, ndoc)), zero), axis=0, keepdims=True)
    placed = jnp.broadcast_to(placed, (ndoc, ndoc))
    placed = jnp.sum(jnp.where(sub == lane, placed, zero), axis=1, keepdims=True)
    placed = jnp.broadcast_to(placed, (ndoc, ndoc))
    starts = jnp.sum(jnp.where(sub < lane, placed, zero), axis=0, keepdims=True)
    first_row = (device * rows).astype(jnp.float32)
    starts = jnp.broadcast_to(starts - first_row, (rows, ndoc))
    token = lax.broadcasted_iota(jnp.int32, (rows, ndoc), 0).astype(jnp.float32)
    begin = jnp.max(jnp.where(starts <= token, starts, -first_row), axis=1, keepdims=True)
    rel_buf[...] = jnp.broadcast_to(begin, (rows, HD))

    q_copy.wait()
    key = lax.broadcasted_iota(jnp.int32, (rows, HD), 1).astype(jnp.float32)
    query = lax.broadcasted_iota(jnp.int32, (rows, HD), 0).astype(jnp.float32)

    def scores(d, h, mask):
        q = jnp.concatenate(
            [q_buf[:, pl.ds(pl.multiple_of((h * group + j) * HD, HD), HD)] for j in range(group)], axis=0)
        s = lax.dot_general(q, kv[d, h, 0], (((1,), (1,)), ((), ())), preferred_element_type=jnp.float32)
        s = jnp.where(mask[None], s.reshape(group, rows, HD), -jnp.inf)
        return s.reshape(group * rows, HD)

    def first(h, mask):
        s = scores(0, h, mask)
        m = jnp.max(s, axis=1, keepdims=True)
        p = jnp.exp2((s - m) * SCALE)
        m_buf[h] = m
        l_buf[h] = jnp.sum(p, axis=1, keepdims=True)
        acc[h] = jnp.dot(p.astype(jnp.bfloat16), kv[0, h, 1], preferred_element_type=jnp.float32)

    def later(d, h, mask):
        s = scores(d, h, mask)
        m_old = m_buf[h]
        m = jnp.maximum(m_old, jnp.max(s, axis=1, keepdims=True))
        p = jnp.exp2((s - m) * SCALE)
        alpha = jnp.exp2((m_old - m) * SCALE)
        total_p = alpha * l_buf[h] + jnp.sum(p, axis=1, keepdims=True)
        mixed = alpha * acc[h] + jnp.dot(p.astype(jnp.bfloat16), kv[d, h, 1], preferred_element_type=jnp.float32)
        return m, total_p, mixed

    own = (key >= rel_buf[...]) & (key <= query)

    @pl.loop(0, kv_heads)
    def _(h):
        first(h, own)

    @pl.loop(1, HOPS)
    def _(d):
        mask = key - (d * rows).astype(jnp.float32) >= rel_buf[...]

        @pl.loop(0, kv_heads)
        def _(h):
            hop(d - 1, h).wait_recv()
            hop(d, h).start()
            m, total_p, mixed = later(d, h, mask)
            m_buf[h] = m
            l_buf[h] = total_p
            acc[h] = mixed

    last = key - float(HOPS * rows) >= rel_buf[...]

    @pl.loop(0, kv_heads)
    def _(h):
        hop(HOPS - 1, h).wait_recv()
        m, total_p, mixed = later(HOPS, h, last)
        out = (mixed / total_p).astype(o_buf.dtype)
        for j in range(group):
            o_buf[:, pl.ds(pl.multiple_of((h * group + j) * HD, HD), HD)] = out[j * rows:(j + 1) * rows]
        give(h).start()

    @pl.loop(0, HOPS)
    def _(d):
        @pl.loop(0, kv_heads)
        def _(h):
            hop(d, h).wait_send()

    @pl.loop(0, kv_heads)
    def _(h):
        give(h).wait()


def solution(mesh):
    sizes = (mesh.shape["outer"], mesh.shape["inner"])

    def shards(queries, keys, values, lengths, pack_order):
        rows = queries.shape[0]
        kv_heads = keys.shape[1] // HD
        group = queries.shape[1] // keys.shape[1]
        ndoc = lengths.shape[0]
        hbm = pl.BlockSpec(memory_space=pltpu.HBM)
        return pl.pallas_call(
            functools.partial(kernel, sizes),
            out_shape=jax.ShapeDtypeStruct(queries.shape, jnp.bfloat16),
            in_specs=[hbm] * 5,
            out_specs=hbm,
            scratch_shapes=[
                pltpu.VMEM((1, ndoc), jnp.int32),
                pltpu.VMEM((1, ndoc), jnp.int32),
                pltpu.VMEM(queries.shape, jnp.bfloat16),
                pltpu.VMEM(queries.shape, jnp.bfloat16),
                pltpu.VMEM((HOPS + 1, kv_heads, 2, rows, HD), jnp.bfloat16),
                pltpu.VMEM((kv_heads, group * rows, HD), jnp.float32),
                pltpu.VMEM((kv_heads, group * rows, 1), jnp.float32),
                pltpu.VMEM((kv_heads, group * rows, 1), jnp.float32),
                pltpu.VMEM((rows, HD), jnp.float32),
                pltpu.SemaphoreType.DMA((2,)),
                pltpu.SemaphoreType.DMA,
                pltpu.SemaphoreType.DMA((kv_heads, 2)),
                pltpu.SemaphoreType.DMA((kv_heads,)),
                pltpu.SemaphoreType.DMA((HOPS, kv_heads)),
                pltpu.SemaphoreType.DMA((HOPS, kv_heads)),
            ],
            compiler_params=pltpu.CompilerParams(
                collective_id=0, has_side_effects=True, vmem_limit_bytes=67043328),
            name="relay_attention",
        )(queries, keys, values, lengths.reshape(1, ndoc), pack_order.reshape(1, ndoc))

    return jax.shard_map(
        shards,
        mesh=mesh,
        in_specs=(P(("outer", "inner"), None),) * 3 + (P(), P()),
        out_specs=P(("outer", "inner"), None),
        check_vma=False,
    )
```

time: 195 us -> 118 us (0.61)
  the two profiles are of different devices: /device:TPU:6 before, /device:TPU:1 now
where the time goes in v1:
time: 118 us
  Pallas kernels  116 us (98%)
  local copies, waits for them, and re-layouts  2.29 us (2%)
    pallas_call x1, Pallas kernels, shards(): pl.pallas_call(functools.partial(kernel, sizes), out_shape=jax.ShapeDtype...  116 us

profile of v1, /device:TPU:1, one launch (start us, length us, event | category | flops | bytes accessed | tf_op | source)
XLA Modules:
  0.0 118.3 jit_solution(10406270023903830589)
XLA Ops:
  0.0 116.0 %relay_attention.1 = bf16[128,4096]{1,0:T(8,128)(2,1)} custom-call(bf16[128,4096]{1,0:T(8,128)(2,1)} %q_hbm.1, bf16[128,1024]{1,0:T(8,128)(2,1)} %k_hbm.1, bf16[128,1024]{1,0:T(8,128)(2,1)} %v_hbm.1, s32[1,256]{1,0:T(1,128)} %bitcast.2, s32[1,256]{1,0:T(1,128)} %bitcast.3), custom_call_target="tpu_custom_call" | custom-call | tf_op jit(solution)/shard_map/relay_attention/pallas_call | solution.py:168
  116.0 2.3 %copy.7 = bf16[128,4096]{1,0:T(8,128)(2,1)} copy(bf16[128,4096]{1,0:T(8,128)(2,1)} %relay_attention.1) | data formatting | bytes 2097152

commit v2 on v1

--- a/solution.py
+++ b/solution.py
@@ -10,12 +10,15 @@
 
 HD = 128
 HOPS = 8
+RING = 32
+LEG = (RING - HOPS) // 2
 MESH = pl.DeviceIdType.MESH
 SCALE = math.log2(math.e) / math.sqrt(HD)
 
 
 def kernel(sizes, q_hbm, k_hbm, v_hbm, len_hbm, ord_hbm, o_hbm,
-           len_ref, ord_ref, q_buf, o_buf, kv, acc, m_buf, l_buf, rel_buf, doc_sem, q_sem, in_sem, out_sem, send_sem, recv_sem):
+           len_ref, ord_ref, q_buf, o_buf, kv, mid_buf, acc, m_buf, l_buf, rel_buf, doc_sem, q_sem, in_sem, out_sem, send_sem, recv_sem,
+           leg_send, leg_recv, back_send, back_recv, word):
     n_outer, n_inner = sizes
     rows = q_hbm.shape[0]
     kv_heads = k_hbm.shape[1] // HD
@@ -24,10 +27,18 @@
     outer, inner = lax.axis_index("outer"), lax.axis_index("inner")
     device = outer * n_inner + inner
     total = n_outer * n_inner
-    after = lax.rem(device + 1, total)
-    before = lax.rem(device + total - 1, total)
-    right = (after // n_inner, lax.rem(after, n_inner))
-    left = (before // n_inner, lax.rem(before, n_inner))
+    z = lax.rem(inner, RING)
+    far = kv_heads - 1
+
+    def place(index):
+        index = lax.rem(index + total, total)
+        return (index // n_inner, lax.rem(index, n_inner))
+
+    right, left = place(device + 1), place(device - 1)
+    first_middle = RING - HOPS - LEG
+    is_source = z >= RING - HOPS
+    is_middle = (z >= first_middle) & (z < first_middle + HOPS)
+    is_start = z < HOPS
 
     def load(h, part):
         source = k_hbm if part == 0 else v_hbm
@@ -43,6 +54,26 @@
             src_ref=kv.at[d, h], dst_ref=kv.at[d + 1, h],
             send_sem=send_sem.at[d, h], recv_sem=recv_sem.at[d, h],
             device_id=right, device_id_type=MESH)
+
+    def leg_one():
+        return pltpu.make_async_remote_copy(
+            src_ref=kv.at[0, far], dst_ref=mid_buf, send_sem=leg_send.at[0], recv_sem=leg_recv,
+            device_id=place(device - LEG), device_id_type=MESH)
+
+    def leg_two():
+        return pltpu.make_async_remote_copy(
+            src_ref=mid_buf, dst_ref=kv.at[HOPS, far], send_sem=leg_send.at[1], recv_sem=back_recv.at[HOPS],
+            device_id=place(device + LEG + HOPS), device_id_type=MESH)
+
+    def back(d):
+        return pltpu.make_async_remote_copy(
+            src_ref=kv.at[d, far], dst_ref=kv.at[d - 1, far], send_sem=back_send.at[d], recv_sem=back_recv.at[d - 1],
+            device_id=left, device_id_type=MESH)
+
+    def arrived(d):
+        return pltpu.make_async_remote_copy(
+            src_ref=kv.at[d, far], dst_ref=kv.at[d, far], send_sem=back_send.at[d], recv_sem=back_recv.at[d],
+            device_id=left, device_id_type=MESH)
 
     @pl.loop(0, kv_heads)
     def _(h):
@@ -57,15 +88,42 @@
     q_copy.start()
 
     barrier = pltpu.get_barrier_semaphore()
-    for neighbour in (left, right):
+
+    def greet(neighbour):
         pl.semaphore_signal(barrier, inc=1, device_id=neighbour, device_id_type=MESH)
-    pl.semaphore_wait(barrier, 2)
-
-    @pl.loop(0, kv_heads)
+
+    greet(left)
+
+    @pl.when(is_start)
+    def _():
+        greet(place(device - HOPS - LEG))
+
+    @pl.when(z < HOPS - 1)
+    def _():
+        greet(right)
+
+    two = is_middle | ((z > 0) & is_start)
+
+    @pl.when(two)
+    def _():
+        pl.semaphore_wait(barrier, 2)
+
+    @pl.when(jnp.logical_not(two))
+    def _():
+        pl.semaphore_wait(barrier, 1)
+
+    load(far, 0).wait()
+    load(far, 1).wait()
+
+    @pl.loop(0, far)
     def _(h):
         load(h, 0).wait()
         load(h, 1).wait()
         hop(0, h).start()
+
+    @pl.when(z < RING - 1)
+    def _():
+        hop(0, far).start()
 
     len_copy.wait()
     ord_copy.wait()
@@ -121,33 +179,112 @@
     def _(h):
         first(h, own)
 
-    @pl.loop(1, HOPS)
-    def _(d):
-        mask = key - (d * rows).astype(jnp.float32) >= rel_buf[...]
-
-        @pl.loop(0, kv_heads)
-        def _(h):
-            hop(d - 1, h).wait_recv()
-            hop(d, h).start()
-            m, total_p, mixed = later(d, h, mask)
-            m_buf[h] = m
-            l_buf[h] = total_p
-            acc[h] = mixed
-
-    last = key - float(HOPS * rows) >= rel_buf[...]
-
-    @pl.loop(0, kv_heads)
-    def _(h):
-        hop(HOPS - 1, h).wait_recv()
-        m, total_p, mixed = later(HOPS, h, last)
+    def keep(d, h, mask):
+        m, total_p, mixed = later(d, h, mask)
+        m_buf[h] = m
+        l_buf[h] = total_p
+        acc[h] = mixed
+
+    def finish(h, total_p, mixed):
         out = (mixed / total_p).astype(o_buf.dtype)
         for j in range(group):
             o_buf[:, pl.ds(pl.multiple_of((h * group + j) * HD, HD), HD)] = out[j * rows:(j + 1) * rows]
         give(h).start()
 
+    def seen(d):
+        return key - (d * rows).astype(jnp.float32) >= rel_buf[...]
+
+    @pl.loop(1, HOPS)
+    def _(d):
+        mask = seen(d)
+
+        @pl.loop(0, far)
+        def _(h):
+            tick = (d - 1) * far + h
+
+            @pl.when((z >= first_middle) & (tick == (z - first_middle) // 2))
+            def _():
+                @pl.when(z > first_middle)
+                def _():
+                    pl.semaphore_wait(word, 1)
+
+                @pl.when(z < RING - 1)
+                def _():
+                    pl.semaphore_signal(word, inc=1, device_id=right, device_id_type=MESH)
+
+                @pl.when(is_source)
+                def _():
+                    leg_one().start()
+
+            hop(d - 1, h).wait_recv()
+            hop(d, h).start()
+            keep(d, h, mask)
+
+            @pl.when(is_middle & (tick == LEG + z - first_middle))
+            def _():
+                leg_one().wait_recv()
+                leg_two().start()
+
+            event = tick - 4 * far
+            turn = (event - 1) // 2
+            e = HOPS - turn
+
+            @pl.when((event >= 1) & (event == turn * 2 + 1) & (e > z))
+            def _():
+                arrived(e).wait_recv()
+
+                @pl.when(z > 0)
+                def _():
+                    back(e).start()
+
+                keep(e, far, seen(e))
+
+        @pl.when(z >= d)
+        def _():
+            hop(d - 1, far).wait_recv()
+
+            @pl.when(z < RING - 1)
+            def _():
+                hop(d, far).start()
+
+            keep(d, far, mask)
+
+    last = seen(jnp.int32(HOPS))
+
+    @pl.loop(0, far)
+    def _(h):
+        hop(HOPS - 1, h).wait_recv()
+        m, total_p, mixed = later(HOPS, h, last)
+        finish(h, total_p, mixed)
+
+    @pl.when(z >= HOPS)
+    def _():
+        hop(HOPS - 1, far).wait_recv()
+        keep(HOPS, far, last)
+
+    finish(far, l_buf[far], acc[far])
+
+    @pl.when(is_source)
+    def _():
+        leg_one().wait_send()
+
+    @pl.when(is_middle)
+    def _():
+        leg_two().wait_send()
+
+    @pl.loop(1, HOPS + 1)
+    def _(d):
+        @pl.when((z > 0) & (d > z))
+        def _():
+            back(d).wait_send()
+
     @pl.loop(0, HOPS)
     def _(d):
-        @pl.loop(0, kv_heads)
+        @pl.when((z >= d) & (z < RING - 1))
+        def _():
+            hop(d, far).wait_send()
+
+        @pl.loop(0, far)
         def _(h):
             hop(d, h).wait_send()
 
@@ -176,6 +313,7 @@
                 pltpu.VMEM(queries.shape, jnp.bfloat16),
                 pltpu.VMEM(queries.shape, jnp.bfloat16),
                 pltpu.VMEM((HOPS + 1, kv_heads, 2, rows, HD), jnp.bfloat16),
+                pltpu.VMEM((2, rows, HD), jnp.bfloat16),
                 pltpu.VMEM((kv_heads, group * rows, HD), jnp.float32),
                 pltpu.VMEM((kv_heads, group * rows, 1), jnp.float32),
                 pltpu.VMEM((kv_heads, group * rows, 1), jnp.float32),
@@ -186,6 +324,11 @@
                 pltpu.SemaphoreType.DMA((kv_heads,)),
                 pltpu.SemaphoreType.DMA((HOPS, kv_heads)),
                 pltpu.SemaphoreType.DMA((HOPS, kv_heads)),
+                pltpu.SemaphoreType.DMA((2,)),
+                pltpu.SemaphoreType.DMA,
+                pltpu.SemaphoreType.DMA((HOPS + 1,)),
+                pltpu.SemaphoreType.DMA((HOPS + 1,)),
+                pltpu.SemaphoreType.REGULAR,
             ],
             compiler_params=pltpu.CompilerParams(
                 collective_id=0, has_side_effects=True, vmem_limit_bytes=67043328),

time: 118 us -> 112 us (0.949)
  Pallas kernels: 116 us -> 110 us
    pallas_call x1, Pallas kernels: 116 us -> 110 us  [shards(): pl.pallas_call(functools.partial(kernel, sizes), out_shape=jax.ShapeDtype...]
where the time goes in v2:
time: 112 us
  Pallas kernels  110 us (98%)
  local copies, waits for them, and re-layouts  2.29 us (2%)
    pallas_call x1, Pallas kernels, shards(): pl.pallas_call(functools.partial(kernel, sizes), out_shape=jax.ShapeDtype...  110 us
    unnamed x1, local copies, waits for them, and re-layouts  2.29 us

profile of v2, /device:TPU:1, one launch (start us, length us, event | category | flops | bytes accessed | tf_op | source)
XLA Modules:
  0.0 111.9 jit_solution(2056005910505852027)
XLA Ops:
  0.0 109.6 %relay_attention.1 = bf16[128,4096]{1,0:T(8,128)(2,1)} custom-call(bf16[128,4096]{1,0:T(8,128)(2,1)} %q_hbm.1, bf16[128,1024]{1,0:T(8,128)(2,1)} %k_hbm.1, bf16[128,1024]{1,0:T(8,128)(2,1)} %v_hbm.1, s32[1,256]{1,0:T(1,128)} %bitcast.2, s32[1,256]{1,0:T(1,128)} %bitcast.3), custom_call_target="tpu_custom_call" | custom-call | tf_op jit(solution)/shard_map/relay_attention/pallas_call | solution.py:305
  109.6 2.3 %copy.7 = bf16[128,4096]{1,0:T(8,128)(2,1)} copy(bf16[128,4096]{1,0:T(8,128)(2,1)} %relay_attention.1) | data formatting | bytes 2097152

commit v3 on v2

--- a/solution.py
+++ b/solution.py
@@ -16,8 +16,8 @@
 SCALE = math.log2(math.e) / math.sqrt(HD)
 
 
-def kernel(sizes, q_hbm, k_hbm, v_hbm, len_hbm, ord_hbm, o_hbm,
-           len_ref, ord_ref, q_buf, o_buf, kv, mid_buf, acc, m_buf, l_buf, rel_buf, doc_sem, q_sem, in_sem, out_sem, send_sem, recv_sem,
+def kernel(sizes, q_hbm, k_hbm, v_hbm, len_hbm, ord_hbm, o_buf,
+           len_ref, ord_ref, q_buf, kv, mid_buf, acc, m_buf, l_buf, rel_buf, doc_sem, q_sem, in_sem, send_sem, recv_sem,
            leg_send, leg_recv, back_send, back_recv, word):
     n_outer, n_inner = sizes
     rows = q_hbm.shape[0]
@@ -44,10 +44,6 @@
         source = k_hbm if part == 0 else v_hbm
         columns = pl.ds(pl.multiple_of(h * HD, HD), HD)
         return pltpu.make_async_copy(source.at[:, columns], kv.at[0, h, part], in_sem.at[h, part])
-
-    def give(h):
-        columns = pl.ds(pl.multiple_of(h * group * HD, group * HD), group * HD)
-        return pltpu.make_async_copy(o_buf.at[:, columns], o_hbm.at[:, columns], out_sem.at[h])
 
     def hop(d, h):
         return pltpu.make_async_remote_copy(
@@ -189,7 +185,6 @@
         out = (mixed / total_p).astype(o_buf.dtype)
         for j in range(group):
             o_buf[:, pl.ds(pl.multiple_of((h * group + j) * HD, HD), HD)] = out[j * rows:(j + 1) * rows]
-        give(h).start()
 
     def seen(d):
         return key - (d * rows).astype(jnp.float32) >= rel_buf[...]
@@ -287,10 +282,6 @@
         @pl.loop(0, far)
         def _(h):
             hop(d, h).wait_send()
-
-    @pl.loop(0, kv_heads)
-    def _(h):
-        give(h).wait()
 
 
 def solution(mesh):
@@ -306,11 +297,10 @@
             functools.partial(kernel, sizes),
             out_shape=jax.ShapeDtypeStruct(queries.shape, jnp.bfloat16),
             in_specs=[hbm] * 5,
-            out_specs=hbm,
+            out_specs=pl.BlockSpec(memory_space=pltpu.VMEM),
             scratch_shapes=[
                 pltpu.VMEM((1, ndoc), jnp.int32),
                 pltpu.VMEM((1, ndoc), jnp.int32),
-                pltpu.VMEM(queries.shape, jnp.bfloat16),
                 pltpu.VMEM(queries.shape, jnp.bfloat16),
                 pltpu.VMEM((HOPS + 1, kv_heads, 2, rows, HD), jnp.bfloat16),
                 pltpu.VMEM((2, rows, HD), jnp.bfloat16),
@@ -321,7 +311,6 @@
                 pltpu.SemaphoreType.DMA((2,)),
                 pltpu.SemaphoreType.DMA,
                 pltpu.SemaphoreType.DMA((kv_heads, 2)),
-                pltpu.SemaphoreType.DMA((kv_heads,)),
                 pltpu.SemaphoreType.DMA((HOPS, kv_heads)),
                 pltpu.SemaphoreType.DMA((HOPS, kv_heads)),
                 pltpu.SemaphoreType.DMA((2,)),
@@ -331,9 +320,9 @@
                 pltpu.SemaphoreType.REGULAR,
             ],
             compiler_params=pltpu.CompilerParams(
-                collective_id=0, has_side_effects=True, vmem_limit_bytes=67043328),
+                collective_id=0, has_side_effects=True, vmem_limit_bytes=50000000),
             name="relay_attention",
-        )(queries, keys, values, lengths.reshape(1, ndoc), pack_order.reshape(1, ndoc))
+        )(*[pltpu.with_memory_space_constraint(x, pltpu.HBM) for x in (queries, keys, values, lengths.reshape(1, ndoc), pack_order.reshape(1, ndoc))])
 
     return jax.shard_map(
         shards,

time: 112 us -> 110 us (0.982)
  local copies, waits for them, and re-layouts: 2.29 us -> 0.97 us
    unnamed x1, local copies, waits for them, and re-layouts: 2.29 us -> 0.97 us
where the time goes in v3:
time: 110 us
  Pallas kernels  109 us (99%)
    pallas_call x1, Pallas kernels, shards(): pl.pallas_call(functools.partial(kernel, sizes), out_shape=jax.ShapeDtype...  109 us

profile of v3, /device:TPU:1, one launch (start us, length us, event | category | flops | bytes accessed | tf_op | source)
XLA Modules:
  0.0 110.3 jit_solution(4420365694220975603)
XLA Ops:
  0.0 109.3 %relay_attention.1 = bf16[128,4096]{1,0:T(8,128)(2,1)S(1)} custom-call(bf16[128,4096]{1,0:T(8,128)(2,1)} %q_hbm.1, bf16[128,1024]{1,0:T(8,128)(2,1)} %k_hbm.1, bf16[128,1024]{1,0:T(8,128)(2,1)} %v_hbm.1, s32[1,256]{1,0:T(1,128)} %bitcast.2, s32[1,256]{1,0:T(1,128)} %bitcast.3), custom_call_target="tpu_custom_call" | custom-call | tf_op jit(solution)/shard_map/relay_attention/pallas_call | solution.py:296
  109.3 1.0 copy.7

commit v4 on v3

--- a/solution.py
+++ b/solution.py
@@ -221,10 +221,10 @@
                 leg_two().start()
 
             event = tick - 4 * far
-            turn = (event - 1) // 2
+            turn = event // 2
             e = HOPS - turn
 
-            @pl.when((event >= 1) & (event == turn * 2 + 1) & (e > z))
+            @pl.when((event >= 0) & (event == turn * 2) & (e > z))
             def _():
                 arrived(e).wait_recv()
 

time: 110 us -> 110 us (level)
  no operation moved by 1% of the time
where the time goes in v4:
time: 110 us
  Pallas kernels  109 us (99%)
    pallas_call x1, Pallas kernels, shards(): pl.pallas_call(functools.partial(kernel, sizes), out_shape=jax.ShapeDtype...  109 us

profile of v4, /device:TPU:1, one launch (start us, length us, event | category | flops | bytes accessed | tf_op | source)
XLA Modules:
  0.0 110.3 jit_solution(6937640498734580748)
XLA Ops:
  0.0 109.3 %relay_attention.1 = bf16[128,4096]{1,0:T(8,128)(2,1)S(1)} custom-call(bf16[128,4096]{1,0:T(8,128)(2,1)} %q_hbm.1, bf16[128,1024]{1,0:T(8,128)(2,1)} %k_hbm.1, bf16[128,1024]{1,0:T(8,128)(2,1)} %v_hbm.1, s32[1,256]{1,0:T(1,128)} %bitcast.2, s32[1,256]{1,0:T(1,128)} %bitcast.3), custom_call_target="tpu_custom_call" | custom-call | tf_op jit(solution)/shard_map/relay_attention/pallas_call | solution.py:296
  109.3 1.0 copy.7
